TPU v7x, 32 devices: a whole 2x2x4 slice. The times are simulated.
32 devices in a mesh: groups: 2 (over x), tok: 16 (over z, y, core).
Axes of the slice: x: 2, y: 2, z: 4, core: 2. Of those that a mesh axis runs over, the one named last changes fastest.
Arguments:
- tokens: bfloat16 [8192, 1024], P(('groups', 'tok')), parts along dimension 0, may hold values from -6 to 6
- norm_gain: float32 [1024], replicated, may hold values from 0.1 to 1.9
- w_qk: bfloat16 [1024, 1024], replicated, may hold values from -0.1875 to 0.1875
- w_v: bfloat16 [1024, 1024], replicated, may hold values from -0.1875 to 0.1875
- cotangent: bfloat16 [8192, 1024], P(('groups', 'tok')), parts along dimension 0, may hold values from -48 to 48
- log_sums: float32 [2, 8, 8192], P(None, None, ('groups', 'tok')), parts along dimension 2, may hold values from 7 to 8
- bucket_order: int32 [2, 8192], P(None, 'groups'), parts along dimension 1, may hold values from 0 to 4095, as said below
- token_position: int32 [2, 8192], P(None, ('groups', 'tok')), parts along dimension 1, may hold values from 0 to 4095, as said below
Outputs:
- d_tokens: bfloat16 [8192, 1024], P(('groups', 'tok')), parts along dimension 0
- d_gain: float32 [2048], P(('groups', 'tok')), parts along dimension 0
- d_wqk: float32 [2048, 1024], P(('groups', 'tok')), parts along dimension 0
- d_wv: float32 [2048, 1024], P(('groups', 'tok')), parts along dimension 0
There are 2 independent parts, one for each index of `groups`. A program takes and returns all parts, laid end to end along the dimension named above; an argument that names none is the same for every part. Nothing has to cross between parts.
Inputs may be any that keep to these rules, and one draw needn't show every extreme that they name: `bucket_order`: each row is a permutation; the 256 hash-sorted positions of one device hold at most 20 tokens of any one device's 256 tokens, and exactly 20 of at least one. token_position[r, bucket_order[r, p]] = p.
All inputs are finite; a program needn't handle non-finite values.
Results may differ from a plain program's by a relative error of at most 0.025.
Values may be sent and summed in bfloat16 or wider, within the bound.
A program may use at most 128 MiB of HBM per device.

v0:
```python
import functools
import math

import jax
import jax.numpy as jnp
from jax import lax
from jax.experimental import pallas as pl
from jax.experimental.pallas import tpu as pltpu
from jax.sharding import PartitionSpec as P

BLOCK = 256
EPS = 1e-06
VMEM_LIMIT = 60 * 1024 * 1024
MESH = pl.DeviceIdType.MESH
F32 = jnp.float32
BF16 = jnp.bfloat16


def whole(count):
    return [pl.BlockSpec(memory_space=pltpu.VMEM)] * count


def dot_nn(a, b):
    return lax.dot_general(a, b, (((1,), (0,)), ((), ())), preferred_element_type=F32)


def dot_nt(a, b):
    return lax.dot_general(a, b, (((1,), (1,)), ((), ())), preferred_element_type=F32)


def dot_tn(a, b):
    return lax.dot_general(a, b, (((0,), (0,)), ((), ())), preferred_element_type=F32)


def params(**more):
    return pltpu.CompilerParams(vmem_limit_bytes=VMEM_LIMIT, **more)


def slot_row(groups, order, stride, cap_offset):
    size = groups.shape[1]
    groups_col = jnp.broadcast_to(groups, (size, size)).T
    order_col = jnp.broadcast_to(order, (size, size)).T
    earlier = (groups_col == groups) & (order_col < order)
    rank = jnp.sum(earlier.astype(F32), axis=0, keepdims=True).astype(jnp.int32)
    return groups * stride + rank + cap_offset


def one_hot_rows(slots, slot_count):
    size = slots.shape[1]
    ids = lax.broadcasted_iota(jnp.int32, (slot_count, size), 0)
    return jnp.where(ids == slots, 1.0, 0.0).astype(BF16)


def home_slots(places, tok_dev, stride, cap_offset):
    return slot_row(lax.div(places, jnp.int32(tok_dev)), places, stride, cap_offset)


def sorted_slots(order, tok_dev, stride, cap_offset):
    position = lax.broadcasted_iota(jnp.int32, order.shape, 1)
    return slot_row(lax.div(order, jnp.int32(tok_dev)), position, stride, cap_offset)


def dispatch_kernel(devices, capacity, chunk, places_ref, tokens_ref, cot_ref, out_ref):
    rounds, tok_dev = places_ref.shape
    for hashing in range(rounds):
        places = places_ref[hashing : hashing + 1, :]
        slots = home_slots(places, tok_dev, chunk, 0)
        rows = dot_nn(one_hot_rows(slots, devices * chunk), tokens_ref[...])
        rows += dot_nn(one_hot_rows(slots + capacity, devices * chunk), cot_ref[...])
        out_ref[hashing] = rows.astype(BF16)


def exchange_kernel(pieces, *refs):
    sources, targets = refs[:pieces], refs[pieces : 2 * pieces]
    send_sem, recv_sem, own_sem = refs[2 * pieces :]
    devices = lax.axis_size("tok")
    me = lax.axis_index("tok")
    barrier = pltpu.get_barrier_semaphore()
    for step in range(1, devices):
        peer = lax.rem(me + step, devices)
        pl.semaphore_signal(barrier, inc=1, device_id={"tok": peer}, device_id_type=MESH)
    own = [
        pltpu.make_async_copy(sources[i].at[me], targets[i].at[me], own_sem.at[i])
        for i in range(pieces)
    ]
    for copy in own:
        copy.start()
    pl.semaphore_wait(barrier, devices - 1)
    copies = []
    for i in range(pieces):
        for step in range(1, devices):
            peer = lax.rem(me + step, devices)
            copy = pltpu.make_async_remote_copy(
                src_ref=sources[i].at[peer],
                dst_ref=targets[i].at[me],
                send_sem=send_sem.at[i, step - 1],
                recv_sem=recv_sem.at[i, step - 1],
                device_id={"tok": peer},
                device_id_type=MESH,
            )
            copy.start()
            copies.append(copy)
    for copy in own:
        copy.wait()
    for copy in copies:
        copy.wait()


def exchange(arrays, collective_id):
    devices = lax.axis_size("tok")
    pieces = len(arrays)
    return pl.pallas_call(
        functools.partial(exchange_kernel, pieces),
        out_shape=[jax.ShapeDtypeStruct(a.shape, a.dtype) for a in arrays],
        in_specs=[pl.BlockSpec(memory_space=pl.ANY)] * pieces,
        out_specs=[pl.BlockSpec(memory_space=pl.ANY)] * pieces,
        scratch_shapes=[
            pltpu.SemaphoreType.DMA((pieces, devices - 1)),
            pltpu.SemaphoreType.DMA((pieces, devices - 1)),
            pltpu.SemaphoreType.DMA((pieces,)),
        ],
        compiler_params=pltpu.CompilerParams(collective_id=collective_id, has_side_effects=True),
    )(*arrays)


def sort_kernel(capacity, chunk, order_ref, arrived_ref, x_ref, g_ref):
    tok_dev = order_ref.shape[2]
    slot_count = arrived_ref.shape[1]
    slots = sorted_slots(order_ref[0], tok_dev, chunk, 0)
    rows = arrived_ref[0]
    x_ref[0] = dot_tn(one_hot_rows(slots, slot_count), rows).astype(BF16)
    g_ref[0] = dot_tn(one_hot_rows(slots + capacity, slot_count), rows).astype(BF16)


def normal_of(x, gain):
    return (x * lax.rsqrt(jnp.mean(x * x, axis=-1, keepdims=True) + EPS) * gain).astype(BF16)


def unit_of(q):
    depth = q.shape[-1]
    scale = lax.rsqrt(jnp.mean(q * q, axis=-1, keepdims=True) + EPS)
    return (q * scale / math.sqrt(depth)).astype(BF16)


def project_kernel(x_ref, gain_ref, qk_ref, v_ref, normal_ref, query_ref, value_ref):
    normal = normal_of(x_ref[0].astype(F32), gain_ref[...])
    normal_ref[0] = normal
    query_ref[0] = dot_nn(normal, qk_ref[...]).astype(BF16)
    value_ref[0] = dot_nn(normal, v_ref[...]).astype(BF16)


def attend_kernel(
    halo_ref, gain_ref, qk_ref, v_ref, query_ref, value_ref, g_ref, sums_ref,
    dq_ref, dk_ref, dv_ref, back_ref, halo_q, halo_v,
):
    heads = sums_ref.shape[1]
    rows, width = query_ref.shape[1:]
    depth = width // heads
    normal = normal_of(halo_ref[0].astype(F32), gain_ref[...])
    halo_q[...] = dot_nn(normal, qk_ref[...]).astype(BF16)
    halo_v[...] = dot_nn(normal, v_ref[...]).astype(BF16)
    sums = sums_ref[0].T
    diagonal = lax.broadcasted_iota(jnp.int32, (rows, rows), 0) == lax.broadcasted_iota(
        jnp.int32, (rows, rows), 1
    )
    for head in range(heads):
        part = slice(head * depth, (head + 1) * depth)
        query = query_ref[0, :, part]
        g = g_ref[0, :, part]
        log_sum = sums[:, head : head + 1]
        keys = [unit_of(halo_q[:, part].astype(F32)), unit_of(query.astype(F32))]
        values = [halo_v[:, part], value_ref[0, :, part]]
        weights = [jnp.exp(dot_nt(query, k) - log_sum) for k in keys]
        weights[1] = jnp.where(diagonal, 0.0, weights[1])
        d_weights = [dot_nt(g, v) for v in values]
        total = jnp.sum(weights[0] * d_weights[0] + weights[1] * d_weights[1], -1, keepdims=True)
        d_scores = [(w * (d - total)).astype(BF16) for w, d in zip(weights, d_weights)]
        low = [w.astype(BF16) for w in weights]
        dq_ref[0, :, part] = dot_nn(d_scores[0], keys[0]) + dot_nn(d_scores[1], keys[1])
        dk_ref[0, :, part] = dot_tn(d_scores[1], query)
        dv_ref[0, :, part] = dot_tn(low[1], g)
        back_ref[0, :, part] = dot_tn(d_scores[0], query).astype(BF16)
        back_ref[0, :, width + head * depth : width + (head + 1) * depth] = dot_tn(
            low[0], g
        ).astype(BF16)


def finish_kernel(
    heads, devices, capacity, chunk, grad_scale,
    order_ref, x_ref, normal_ref, query_ref, dq_ref, dk_ref, dv_ref, back_ref, qk_ref, v_ref,
    weights_ref, out_ref, gain_ref, query_low, value_low, rows_low,
):
    rounds, rows, width = query_ref.shape
    depth = width // heads
    gain = jnp.zeros((1, width), F32)
    for hashing in range(rounds):
        span = slice(hashing * rows, (hashing + 1) * rows)
        for head in range(heads):
            part = slice(head * depth, (head + 1) * depth)
            q = query_ref[hashing, :, part].astype(F32)
            dk = dk_ref[hashing, :, part] + back_ref[hashing, :, part].astype(F32)
            scale = lax.rsqrt(jnp.mean(q * q, axis=-1, keepdims=True) + EPS)
            along = jnp.mean(q * dk, axis=-1, keepdims=True)
            pulled = (dk * scale - q * (scale * scale * scale * along)) / math.sqrt(depth)
            query_low[span, part] = (dq_ref[hashing, :, part] + pulled).astype(BF16)
        value_low[span, :] = (
            dv_ref[hashing] + back_ref[hashing, :, width:].astype(F32)
        ).astype(BF16)
        d_normal = dot_nt(query_low[span, :], qk_ref[...]) + dot_nt(value_low[span, :], v_ref[...])
        x = x_ref[hashing].astype(F32)
        scaled = x * lax.rsqrt(jnp.mean(x * x, axis=-1, keepdims=True) + EPS)
        gain += jnp.sum(d_normal * scaled, axis=0, keepdims=True)
        rows_low[span, :] = d_normal.astype(BF16)
    gain_ref[...] = gain * grad_scale
    normal = normal_ref[...].reshape(rounds * rows, width)
    weights_ref[:, :width] = (dot_tn(normal, query_low[...]) * grad_scale).astype(BF16)
    weights_ref[:, width:] = (dot_tn(normal, value_low[...]) * grad_scale).astype(BF16)
    out = jnp.zeros((devices * chunk, width), F32)
    for hashing in range(rounds):
        slots = sorted_slots(order_ref[hashing], rows, chunk, hashing * capacity)
        out += dot_nn(
            one_hot_rows(slots, devices * chunk), rows_low[hashing * rows : (hashing + 1) * rows, :]
        )
    out_ref[...] = out.astype(BF16)


def home_kernel(capacity, chunk, places_ref, back_ref, tokens_ref, gain_ref, parts_ref, out_ref, total_ref):
    rounds, tok_dev = places_ref.shape
    slot_count = back_ref.shape[0]
    picks = None
    for hashing in range(rounds):
        slots = home_slots(places_ref[hashing : hashing + 1, :], tok_dev, chunk, hashing * capacity)
        ones = one_hot_rows(slots, slot_count)
        picks = ones if picks is None else picks + ones
    d_normal = dot_tn(picks, back_ref[...])
    x = tokens_ref[...].astype(F32)
    scale = lax.rsqrt(jnp.mean(x * x, axis=-1, keepdims=True) + EPS)
    t = d_normal * gain_ref[...]
    along = jnp.mean(x * t, axis=-1, keepdims=True)
    out_ref[...] = (t * scale - x * (scale * scale * scale * along)).astype(BF16)
    total_ref[...] = jnp.sum(parts_ref[:, 0, :], axis=0, keepdims=True)


def per_device(tokens, norm_gain, w_qk, w_v, cotangent, log_sums, bucket_order, token_position):
    devices = lax.axis_size("tok")
    me = lax.axis_index("tok")
    tok_dev, width = tokens.shape
    rounds, seq_len = bucket_order.shape
    heads = log_sums.shape[1]
    assert tok_dev == BLOCK
    capacity = 5 * tok_dev // (4 * devices)
    kinds = max(2, rounds)
    chunk = -(-kinds * capacity // 8) * 8
    slots = devices * chunk
    grad_scale = 1.0 / math.sqrt(seq_len)
    gain_row = norm_gain.reshape(1, width)
    my_order = lax.dynamic_slice_in_dim(bucket_order, me * tok_dev, tok_dev, axis=1).reshape(
        rounds, 1, tok_dev
    )
    round_rows = jax.ShapeDtypeStruct((rounds, tok_dev, width), BF16)
    round_rows_f = jax.ShapeDtypeStruct((rounds, tok_dev, width), F32)

    def per_round(*shape):
        return pl.BlockSpec((1,) + shape, lambda r: (r, 0, 0))

    def shared(*shape):
        return pl.BlockSpec(shape, lambda r: (0, 0))

    row_spec = per_round(tok_dev, width)

    outbound = pl.pallas_call(
        functools.partial(dispatch_kernel, devices, capacity, chunk),
        out_shape=jax.ShapeDtypeStruct((rounds, slots, width), BF16),
        in_specs=whole(3),
        out_specs=whole(1)[0],
        compiler_params=params(),
        name="dispatch",
    )(token_position, tokens, cotangent)
    arrived = exchange(
        [outbound[r].reshape(devices, chunk, width) for r in range(rounds)], collective_id=0
    )
    arrived = jnp.stack([a.reshape(slots, width) for a in arrived])
    sorted_x, sorted_g = pl.pallas_call(
        functools.partial(sort_kernel, capacity, chunk),
        grid=(rounds,),
        out_shape=[round_rows, round_rows],
        in_specs=[per_round(1, tok_dev), per_round(slots, width)],
        out_specs=[row_spec, row_spec],
        compiler_params=params(),
        name="sort",
    )(my_order, arrived)
    route = [(i, (i + 1) % devices) for i in range(devices)]
    halo_x = lax.ppermute(sorted_x, "tok", route)
    normal, query, value = pl.pallas_call(
        project_kernel,
        grid=(rounds,),
        out_shape=[round_rows] * 3,
        in_specs=[row_spec, shared(1, width), shared(width, width), shared(width, width)],
        out_specs=[row_spec] * 3,
        compiler_params=params(),
        name="project",
        cost_estimate=pl.CostEstimate(
            flops=4 * rounds * tok_dev * width * width,
            bytes_accessed=4 * width * width + 8 * rounds * tok_dev * width,
            transcendentals=0,
        ),
    )(sorted_x, gain_row, w_qk, w_v)
    dq, dk, dv, back = pl.pallas_call(
        attend_kernel,
        grid=(rounds,),
        out_shape=[round_rows_f] * 3
        + [jax.ShapeDtypeStruct((rounds, tok_dev, 2 * width), BF16)],
        in_specs=[
            row_spec, shared(1, width), shared(width, width), shared(width, width),
            row_spec, row_spec, row_spec, per_round(heads, tok_dev),
        ],
        out_specs=[row_spec] * 3 + [per_round(tok_dev, 2 * width)],
        scratch_shapes=[pltpu.VMEM((tok_dev, width), BF16)] * 2,
        compiler_params=params(),
        name="attend",
    )(halo_x, gain_row, w_qk, w_v, query, value, sorted_g, log_sums)
    returned = lax.ppermute(back, "tok", [(b, a) for a, b in route])
    weights, rows_out, gain_part = pl.pallas_call(
        functools.partial(finish_kernel, heads, devices, capacity, chunk, grad_scale),
        out_shape=[
            jax.ShapeDtypeStruct((width, 2 * width), BF16),
            jax.ShapeDtypeStruct((slots, width), BF16),
            jax.ShapeDtypeStruct((1, width), F32),
        ],
        in_specs=whole(10),
        out_specs=whole(3),
        scratch_shapes=[pltpu.VMEM((rounds * tok_dev, width), BF16)] * 3,
        compiler_params=params(),
        name="finish",
    )(my_order, sorted_x, normal, query, dq, dk, dv, returned, w_qk, w_v)
    grads = lax.psum_scatter(weights, "tok", scatter_dimension=0, tiled=True).astype(F32)
    own = width // devices
    gain_slices = jnp.pad(gain_part.reshape(devices, 1, own), ((0, 0), (0, 7), (0, 128 - own)))
    rows_back, gain_back = exchange(
        [rows_out.reshape(devices, chunk, width), gain_slices], collective_id=1
    )
    d_tokens, d_gain = pl.pallas_call(
        functools.partial(home_kernel, capacity, chunk),
        out_shape=[
            jax.ShapeDtypeStruct((tok_dev, width), BF16),
            jax.ShapeDtypeStruct((1, 128), F32),
        ],
        in_specs=whole(5),
        out_specs=whole(2),
        compiler_params=params(),
        name="home",
    )(token_position, rows_back.reshape(slots, width), tokens, gain_row, gain_back)
    return (d_tokens, d_gain[0, :own], grads[:, :width], grads[:, width:])


def solution(mesh):
    in_specs = (
        P(("groups", "tok"), None),
        P(),
        P(),
        P(),
        P(("groups", "tok"), None),
        P(None, None, ("groups", "tok")),
        P(None, "groups"),
        P(None, ("groups", "tok")),
    )
    out_specs = (
        P(("groups", "tok"), None),
        P(("groups", "tok")),
        P(("groups", "tok"), None),
        P(("groups", "tok"), None),
    )
    return jax.shard_map(
        per_device, mesh=mesh, in_specs=in_specs, out_specs=out_specs, check_vma=False
    )
```

profile of v0, /device:TPU:26, one launch (start us, length us, event | category | flops | bytes accessed | tf_op | source)
XLA Modules:
  0.0 245.6 jit_solution(14699712660074012326)
XLA Ops:
  7.2 0.0 copy-start
  7.2 0.0 reduce-scatter.2.cloned.1.call-start
  7.2 0.7 copy-done
  7.9 0.6 reshape.23.order_ref
  8.5 4.4 %dispatch.1 = bf16[2,640,1024]{2,1,0:T(8,128)(2,1)} custom-call(s32[2,256]{1,0:T(2,128)} %places_ref.3, bf16[256,1024]{1,0:T(8,128)(2,1)} %tokens_ref.3, bf16[256,1024]{1,0:T(8,128)(2,1)} %cot_ref.1), custom_call_target="tpu_custom_call" | custom-call | tf_op jit(solution)/shard_map/dispatch/pallas_call | solution.py:271
  12.9 3.5 %fusion = (bf16[1,640,1024]{2,1,0:T(8,128)(2,1)}, bf16[1,640,1024]{2,1,0:T(8,128)(2,1)}) fusion(bf16[2,640,1024]{2,1,0:T(8,128)(2,1)} %dispatch.1), kind=kLoop, calls=%fused_computation.3 | loop fusion | bytes 5242880 | tf_op jit(solution)/shard_map/slice | solution.py:280
  16.4 57.3 %shard_map.111 = (bf16[16,40,1024]{2,1,0:T(8,128)(2,1)}, bf16[16,40,1024]{2,1,0:T(8,128)(2,1)}) custom-call(bf16[16,40,1024]{2,1,0:T(8,128)(2,1)} %bitcast.10, bf16[16,40,1024]{2,1,0:T(8,128)(2,1)} %bitcast.9), custom_call_target="tpu_custom_call" | custom-call | tf_op jit(solution)/shard_map/pallas_call | solution.py:112
  73.6 3.5 %pad_maximum_fusion.arrived_ref = bf16[2,640,1024]{2,1,0:T(8,128)(2,1)} fusion(bf16[1,640,1024]{2,1,0:T(8,128)(2,1)} %bitcast.12, bf16[1,640,1024]{2,1,0:T(8,128)(2,1)} %bitcast.11), kind=kLoop, calls=%fused_computation | loop fusion | flops 1310720 | bytes 5242880 | tf_op jit(solution)/shard_map/stack | solution.py:282
  77.1 4.5 %sort.1 = (bf16[2,256,1024]{2,1,0:T(8,128)(2,1)}, bf16[2,256,1024]{2,1,0:T(8,128)(2,1)}) custom-call(s32[2,1,256]{2,1,0:T(1,128)} %reshape.23.order_ref, bf16[2,640,1024]{2,1,0:T(8,128)(2,1)} %pad_maximum_fusion.arrived_ref), custom_call_target="tpu_custom_call" | custom-call | tf_op jit(solution)/shard_map/sort/pallas_call | solution.py:283
  81.6 1.6 collective-permute-start
  83.2 6.0 %project.1 = (bf16[2,256,1024]{2,1,0:T(8,128)(2,1)}, bf16[2,256,1024]{2,1,0:T(8,128)(2,1)}, bf16[2,256,1024]{2,1,0:T(8,128)(2,1)}) custom-call(bf16[2,256,1024]{2,1,0:T(8,128)(2,1)} %get-tuple-element.24.x_ref, f32[1,1024]{1,0:T(1,128)} %bitcast.15, bf16[1024,1024]{1,0:T(8,128)(2,1)} %qk_ref.5, bf16[1024,1024]{1,0:T(8,128)(2,1)} %v_ref.5), custom_call_target="tpu_custom_call" | custom-call | flops 2147483648 | bytes 8388608 | tf_op jit(solution)/shard_map/project/pallas_call | solution.py:294
  89.2 8.2 %collective-permute-done.halo_ref = bf16[2,256,1024]{2,1,0:T(8,128)(2,1)S(1)} collective-permute-done((bf16[2,256,1024]{2,1,0:T(8,128)(2,1)}, bf16[2,256,1024]{2,1,0:T(8,128)(2,1)S(1)}, u32[]{:S(2)}, u32[]{:S(2)}) %collective-permute-start) | collective-permute-done | bytes 1048608 | tf_op jit(solution)/shard_map/ppermute | solution.py:293
  97.3 0.0 copy-start.2
  97.3 1.0 copy-done.2
  98.3 18.8 %attend.1 = (f32[2,256,1024]{2,1,0:T(8,128)}, f32[2,256,1024]{2,1,0:T(8,128)}, f32[2,256,1024]{2,1,0:T(8,128)}, bf16[2,256,2048]{2,1,0:T(8,128)(2,1)}) custom-call(bf16[2,256,1024]{2,1,0:T(8,128)(2,1)} %copy-done.2, f32[1,1024]{1,0:T(1,128)} %bitcast.16, bf16[1024,1024]{1,0:T(8,128)(2,1)} %qk_ref.5, bf16[1024,1024]{1,0:T(8,128)(2,1)} %v_ref.5, ...), custom_call_target="tpu_custom_call" | custom-call | tf_op jit(solution)/shard_map/attend/pallas_call | solution.py:308
  117.1 0.1 collective-permute-start.1
  117.2 23.9 %collective-permute-done.1.back_ref = bf16[2,256,2048]{2,1,0:T(8,128)(2,1)S(1)} collective-permute-done((bf16[2,256,2048]{2,1,0:T(8,128)(2,1)}, bf16[2,256,2048]{2,1,0:T(8,128)(2,1)S(1)}, u32[]{:S(2)}, u32[]{:S(2)}) %collective-permute-start.1) | collective-permute-done | bytes 2097184 | tf_op jit(solution)/shard_map/ppermute | solution.py:322
  141.1 0.0 copy-start.1
  141.1 1.3 copy-done.1
  142.4 13.1 %finish.1 = (bf16[1024,2048]{1,0:T(8,128)(2,1)}, bf16[640,1024]{1,0:T(8,128)(2,1)}, f32[1,1024]{1,0:T(1,128)}) custom-call(s32[2,1,256]{2,1,0:T(1,128)} %reshape.23.order_ref, bf16[2,256,1024]{2,1,0:T(8,128)(2,1)} %get-tuple-element.24.x_ref, bf16[2,256,1024]{2,1,0:T(8,128)(2,1)} %get-tuple-element.25.normal_ref, ...), custom_call_target="tpu_custom_call" | custom-call | tf_op jit(solution)/shard_map/finish/pallas_call | solution.py:323
  155.6 0.0 copy-start.3
  155.6 0.0 reduce-scatter.2.cloned.1.call-update
  155.6 0.5 broadcast.5
  156.1 0.1 copy-done.3
  156.2 0.7 reduce.3
  156.9 0.1 reshape.26
  157.0 0.6 pad.4.refs_1_
  157.6 52.3 %shard_map.112 = (bf16[16,40,1024]{2,1,0:T(8,128)(2,1)}, f32[16,8,128]{2,1,0:T(8,128)}) custom-call(bf16[16,40,1024]{2,1,0:T(8,128)(2,1)} %bitcast.13, f32[16,8,128]{2,1,0:T(8,128)} %pad.4.refs_1_), custom_call_target="tpu_custom_call" | custom-call | tf_op jit(solution)/shard_map/pallas_call | solution.py:112
  210.0 3.3 %home.1 = (bf16[256,1024]{1,0:T(8,128)(2,1)}, f32[1,128]{1,0:T(1,128)}) custom-call(s32[2,256]{1,0:T(2,128)} %places_ref.3, bf16[640,1024]{1,0:T(8,128)(2,1)} %bitcast.14, bf16[256,1024]{1,0:T(8,128)(2,1)} %tokens_ref.3, f32[1,1024]{1,0:T(1,128)} %bitcast.17, f32[16,8,128]{2,1,0:T(8,128)} %get-tuple-element.36.parts_ref), custom_call_target="tpu_custom_call" | custom-call | tf_op jit(solution)/shard_map/home/pallas_call | solution.py:342
  213.2 1.2 slice_bitcast_fusion
  214.4 22.5 %reduce-scatter.2.cloned.1.call-done = bf16[64,2048]{1,0:T(8,128)(2,1)} async-done(((bf16[1024,2048]{1,0:T(8,128)(2,1)}), bf16[64,2048]{1,0:T(8,128)(2,1)}) %reduce-scatter.2.cloned.1.call-update) | async-done | bytes 262160 | tf_op jit(solution)/shard_map/reduce_scatter | solution.py:336
  236.9 1.8 fusion.1
  (1 shorter events, 0.0 us)
Async XLA Ops:
  7.2 0.8 copy-start
  7.2 229.7 %reduce-scatter.2.cloned.1.call-start = ((), (), s32[]{:S(2)}) async-start(), calls=%async_computation.1 | async-start | bytes 4456448 | tf_op jit(solution)/shard_map/reduce_scatter | solution.py:336
  81.6 15.7 %collective-permute-start = (bf16[2,256,1024]{2,1,0:T(8,128)(2,1)}, bf16[2,256,1024]{2,1,0:T(8,128)(2,1)S(1)}, u32[]{:S(2)}, u32[]{:S(2)}) collective-permute-start(bf16[2,256,1024]{2,1,0:T(8,128)(2,1)} %get-tuple-element.24.x_ref), channel_id=1, source_target_pairs={{0,1},{1,2},{2,3},{3,4},{4,5},{5,6},{6,7},{7,8},{8,9},{9,10},{10,1... | collective-permute-start | bytes 3145736 | tf_op jit(solution)/shard_map/ppermute | solution.py:293
  97.3 1.0 copy-start.2
  117.1 24.0 %collective-permute-start.1 = (bf16[2,256,2048]{2,1,0:T(8,128)(2,1)}, bf16[2,256,2048]{2,1,0:T(8,128)(2,1)S(1)}, u32[]{:S(2)}, u32[]{:S(2)}) collective-permute-start(bf16[2,256,2048]{2,1,0:T(8,128)(2,1)} %get-tuple-element.32), channel_id=1, source_target_pairs={{1,0},{2,1},{3,2},{4,3},{5,4},{6,5},{7,6},{8,7},{9,8},{10,9},{11,1... | collective-permute-start | bytes 6291464 | tf_op jit(solution)/shard_map/ppermute | solution.py:322
  141.1 1.3 copy-start.1
  155.6 0.7 copy-start.3
Sparse Core Ops, SparseCore 0:
  155.7 81.1 reduce-scatter.1
where the time goes:
time: 249 us; the launch traced here: 246 us
  Pallas kernels  160 us (64%)
  waiting for transfers between devices  54.5 us (22%)
  between operations  14.1 us (6%)
  local copies, waits for them, and re-layouts  11.4 us (5%)
  other arithmetic  4.12 us (2%)
    pallas_call x2, Pallas kernels, exchange(): pl.pallas_call(functools.partial(exchange_kernel, pieces), out_shape=[jax...  110 us
    ppermute x1, waiting for transfers between devices, per_device(): returned = lax.ppermute(back, 'tok', [(b, a) for a, b in route])  23.9 us
    reduce_scatter x1, waiting for transfers between devices, per_device(): lax.psum_scatter(weights, 'tok', scatter_dimension=0, tiled=True)  22.5 us
    pallas_call x1, Pallas kernels, per_device(): pl.pallas_call(attend_kernel, grid=(rounds,), out_shape=[round_rows_f] *...  18.8 us
    pallas_call x1, Pallas kernels, per_device(): pl.pallas_call(functools.partial(finish_kernel, heads, devices, capacity,...  13.1 us
    ppermute x1, waiting for transfers between devices, per_device(): halo_x = lax.ppermute(sorted_x, 'tok', route)  8.15 us
    pallas_call x1, Pallas kernels, per_device(): pl.pallas_call(project_kernel, grid=(rounds,), out_shape=[round_rows] * 3...  5.98 us
  transfers between devices with their start and end apart: 3, of which 3 were waited for; matrix products, arithmetic and copies ran while one was open for 1% of the time, Pallas kernels for 25%

commit v1 on v0

v1 whole, which is shorter than its diff:
```python
import functools
import math

import jax
import jax.numpy as jnp
from jax import lax
from jax.experimental import pallas as pl
from jax.experimental.pallas import tpu as pltpu
from jax.sharding import PartitionSpec as P

BLOCK = 256
EPS = 1e-06
VMEM_LIMIT = 60 * 1024 * 1024
MESH = pl.DeviceIdType.MESH
F32 = jnp.float32
BF16 = jnp.bfloat16


def whole(count):
    return [pl.BlockSpec(memory_space=pltpu.VMEM)] * count


def dot_nn(a, b):
    return lax.dot_general(a, b, (((1,), (0,)), ((), ())), preferred_element_type=F32)


def dot_nt(a, b):
    return lax.dot_general(a, b, (((1,), (1,)), ((), ())), preferred_element_type=F32)


def dot_tn(a, b):
    return lax.dot_general(a, b, (((0,), (0,)), ((), ())), preferred_element_type=F32)


def params(**more):
    return pltpu.CompilerParams(vmem_limit_bytes=VMEM_LIMIT, **more)


def slot_row(groups, order, stride, cap_offset):
    size = groups.shape[1]
    groups_col = jnp.broadcast_to(groups, (size, size)).T
    order_col = jnp.broadcast_to(order, (size, size)).T
    earlier = (groups_col == groups) & (order_col < order)
    rank = jnp.sum(earlier.astype(F32), axis=0, keepdims=True).astype(jnp.int32)
    return groups * stride + rank + cap_offset


def one_hot_rows(slots, slot_count):
    size = slots.shape[1]
    ids = lax.broadcasted_iota(jnp.int32, (slot_count, size), 0)
    return jnp.where(ids == slots, 1.0, 0.0).astype(BF16)


def home_slots(places, tok_dev, stride, cap_offset):
    return slot_row(lax.div(places, jnp.int32(tok_dev)), places, stride, cap_offset)


def sorted_slots(order, tok_dev, stride, cap_offset):
    position = lax.broadcasted_iota(jnp.int32, order.shape, 1)
    return slot_row(lax.div(order, jnp.int32(tok_dev)), position, stride, cap_offset)


def dispatch_kernel(devices, capacity, chunk, places_ref, tokens_ref, cot_ref, *out_refs):
    rounds, tok_dev = places_ref.shape
    for hashing in range(rounds):
        places = places_ref[hashing : hashing + 1, :]
        slots = home_slots(places, tok_dev, chunk, 0)
        rows = dot_nn(one_hot_rows(slots, devices * chunk), tokens_ref[...])
        rows += dot_nn(one_hot_rows(slots + capacity, devices * chunk), cot_ref[...])
        out_refs[hashing][...] = rows.astype(BF16)


def exchange_kernel(pieces, *refs):
    sources, targets = refs[:pieces], refs[pieces : 2 * pieces]
    send_sem, recv_sem, own_sem = refs[2 * pieces :]
    devices = lax.axis_size("tok")
    me = lax.axis_index("tok")
    barrier = pltpu.get_barrier_semaphore()
    for step in range(1, devices):
        peer = lax.rem(me + step, devices)
        pl.semaphore_signal(barrier, inc=1, device_id={"tok": peer}, device_id_type=MESH)
    own = [
        pltpu.make_async_copy(sources[i].at[me], targets[i].at[me], own_sem.at[i])
        for i in range(pieces)
    ]
    for copy in own:
        copy.start()
    pl.semaphore_wait(barrier, devices - 1)
    copies = []
    for i in range(pieces):
        for step in range(1, devices):
            peer = lax.rem(me + step, devices)
            copy = pltpu.make_async_remote_copy(
                src_ref=sources[i].at[peer],
                dst_ref=targets[i].at[me],
                send_sem=send_sem.at[i, step - 1],
                recv_sem=recv_sem.at[i, step - 1],
                device_id={"tok": peer},
                device_id_type=MESH,
            )
            copy.start()
            copies.append(copy)
    for copy in own:
        copy.wait()
    for copy in copies:
        copy.wait()


def exchange(arrays, collective_id):
    devices = lax.axis_size("tok")
    pieces = len(arrays)
    return pl.pallas_call(
        functools.partial(exchange_kernel, pieces),
        out_shape=[jax.ShapeDtypeStruct(a.shape, a.dtype) for a in arrays],
        in_specs=[pl.BlockSpec(memory_space=pl.ANY)] * pieces,
        out_specs=[pl.BlockSpec(memory_space=pl.ANY)] * pieces,
        scratch_shapes=[
            pltpu.SemaphoreType.DMA((pieces, devices - 1)),
            pltpu.SemaphoreType.DMA((pieces, devices - 1)),
            pltpu.SemaphoreType.DMA((pieces,)),
        ],
        compiler_params=pltpu.CompilerParams(collective_id=collective_id, has_side_effects=True),
    )(*arrays)


def normal_of(x, gain):
    return (x * lax.rsqrt(jnp.mean(x * x, axis=-1, keepdims=True) + EPS) * gain).astype(BF16)


def unit_of(q):
    depth = q.shape[-1]
    scale = lax.rsqrt(jnp.mean(q * q, axis=-1, keepdims=True) + EPS)
    return (q * scale / math.sqrt(depth)).astype(BF16)


def core_kernel(heads, capacity, chunk, ahead, grad_scale, *refs):
    rounds = refs[0].shape[0]
    order_ref, gain_ref, qk_ref, v_ref, sums_ref = refs[:5]
    outgoing = refs[5 : 5 + rounds]
    weights_ref, out_ref, gain_out = refs[5 + rounds : 8 + rounds]
    (
        arrived, sorted_x, sorted_g, halo_x, normal, query, value, halo_q, halo_v,
        d_query, d_key, d_value, back_out, back_in, query_low, value_low, rows_low, total,
        send_sem, recv_sem, own_sem, halo_sem, back_sem,
    ) = refs[8 + rounds :]
    devices = lax.axis_size("tok")
    me = lax.axis_index("tok")
    right, left = lax.rem(me + 1, devices), lax.rem(me + devices - 1, devices)
    rows, width = sorted_x.shape[1:]
    depth = width // heads
    slot_count = devices * chunk
    parts = [slice(head * depth, (head + 1) * depth) for head in range(heads)]

    barrier = pltpu.get_barrier_semaphore()
    for step in range(1, devices):
        peer = lax.rem(me + step, devices)
        pl.semaphore_signal(barrier, inc=1, device_id={"tok": peer}, device_id_type=MESH)
    own = [
        pltpu.make_async_copy(outgoing[r].at[me], arrived.at[r, me], own_sem.at[r])
        for r in range(rounds)
    ]
    for copy in own:
        copy.start()
    pl.semaphore_wait(barrier, devices - 1)

    def piece(r, step):
        peer = lax.rem(me + step, devices)
        return pltpu.make_async_remote_copy(
            src_ref=outgoing[r].at[peer],
            dst_ref=arrived.at[r, me],
            send_sem=send_sem.at[r, step - 1],
            recv_sem=recv_sem.at[r, step - 1],
            device_id={"tok": peer},
            device_id_type=MESH,
        )

    pieces = [[piece(r, step) for step in range(1, devices)] for r in range(rounds)]
    halos = [
        pltpu.make_async_remote_copy(
            src_ref=sorted_x.at[r],
            dst_ref=halo_x.at[r],
            send_sem=halo_sem.at[0, r],
            recv_sem=halo_sem.at[1, r],
            device_id={"tok": right},
            device_id_type=MESH,
        )
        for r in range(rounds)
    ]
    backs = [
        pltpu.make_async_remote_copy(
            src_ref=back_out.at[r],
            dst_ref=back_in.at[r],
            send_sem=back_sem.at[0, r],
            recv_sem=back_sem.at[1, r],
            device_id={"tok": left},
            device_id_type=MESH,
        )
        for r in range(rounds)
    ]
    for copy in pieces[0]:
        copy.start()

    def sort(r):
        slots = sorted_slots(order_ref[r], rows, chunk, 0)
        data = arrived[r].reshape(slot_count, width)
        sorted_x[r] = dot_tn(one_hot_rows(slots, slot_count), data).astype(BF16)
        sorted_g[r] = dot_tn(one_hot_rows(slots + capacity, slot_count), data).astype(BF16)

    def project(r):
        normal[r] = normal_of(sorted_x[r].astype(F32), gain_ref[...])
        query[r] = dot_nn(normal[r], qk_ref[...]).astype(BF16)
        value[r] = dot_nn(normal[r], v_ref[...]).astype(BF16)

    def attend(r):
        behind = normal_of(halo_x[r].astype(F32), gain_ref[...])
        halo_q[...] = dot_nn(behind, qk_ref[...]).astype(BF16)
        halo_v[...] = dot_nn(behind, v_ref[...]).astype(BF16)
        sums = sums_ref[r].T
        diagonal = lax.broadcasted_iota(jnp.int32, (rows, rows), 0) == lax.broadcasted_iota(
            jnp.int32, (rows, rows), 1
        )
        for head, part in enumerate(parts):
            q = query[r, :, part]
            g = sorted_g[r, :, part]
            log_sum = sums[:, head : head + 1]
            keys = [unit_of(halo_q[:, part].astype(F32)), unit_of(q.astype(F32))]
            values = [halo_v[:, part], value[r, :, part]]
            weights = [jnp.exp(dot_nt(q, k) - log_sum) for k in keys]
            weights[1] = jnp.where(diagonal, 0.0, weights[1])
            d_weights = [dot_nt(g, v) for v in values]
            delta = jnp.sum(
                weights[0] * d_weights[0] + weights[1] * d_weights[1], -1, keepdims=True
            )
            d_scores = [(w * (d - delta)).astype(BF16) for w, d in zip(weights, d_weights)]
            low = [w.astype(BF16) for w in weights]
            back_out[r, :, part] = dot_tn(d_scores[0], q).astype(BF16)
            back_out[r, :, slice(width + part.start, width + part.stop)] = dot_tn(
                low[0], g
            ).astype(BF16)
            d_query[r, :, part] = dot_nn(d_scores[0], keys[0]) + dot_nn(d_scores[1], keys[1])
            d_key[r, :, part] = dot_tn(d_scores[1], q)
            d_value[r, :, part] = dot_tn(low[1], g)

    def finish(r):
        for part in parts:
            q = query[r, :, part].astype(F32)
            dk = d_key[r, :, part] + back_in[r, :, part].astype(F32)
            scale = lax.rsqrt(jnp.mean(q * q, axis=-1, keepdims=True) + EPS)
            along = jnp.mean(q * dk, axis=-1, keepdims=True)
            pulled = (dk * scale - q * (scale * scale * scale * along)) / math.sqrt(depth)
            query_low[:, part] = (d_query[r, :, part] + pulled).astype(BF16)
        value_low[...] = (d_value[r] + back_in[r, :, width:].astype(F32)).astype(BF16)
        d_normal = dot_nt(query_low[...], qk_ref[...]) + dot_nt(value_low[...], v_ref[...])
        x = sorted_x[r].astype(F32)
        scaled = x * lax.rsqrt(jnp.mean(x * x, axis=-1, keepdims=True) + EPS)
        rows_low[r] = d_normal.astype(BF16)
        for low, columns in (
            (query_low, slice(0, width)),
            (value_low, slice(width, 2 * width)),
        ):
            grad = dot_tn(normal[r], low[...])
            if r > 0:
                grad += total[:, columns]
            if r < rounds - 1:
                total[:, columns] = grad
            else:
                weights_ref[:, columns] = (grad * grad_scale).astype(BF16)
        return jnp.sum(d_normal * scaled, axis=0, keepdims=True)

    for r in range(rounds):
        if r + 1 < rounds:
            for copy in pieces[r + 1][:ahead]:
                copy.start()
        own[r].wait()
        for copy in pieces[r]:
            copy.wait_recv()
        sort(r)
        halos[r].start()
        if r + 1 < rounds:
            for copy in pieces[r + 1][ahead:]:
                copy.start()
        project(r)
        halos[r].wait_recv()
        attend(r)
        backs[r].start()
    gain_total = jnp.zeros((1, width), F32)
    for r in range(rounds):
        backs[r].wait_recv()
        gain_total += finish(r)
    gain_total = gain_total * grad_scale
    share = width // devices
    gain_out[...] = jnp.zeros(gain_out.shape, F32)
    for device in range(devices):
        gain_out[device, 0:1, 0:share] = gain_total[:, device * share : (device + 1) * share]
    out = jnp.zeros((slot_count, width), F32)
    for r in range(rounds):
        slots = sorted_slots(order_ref[r], rows, chunk, r * capacity)
        out += dot_nn(one_hot_rows(slots, slot_count), rows_low[r])
    out_ref[...] = out.astype(BF16)
    for r in range(rounds):
        for copy in pieces[r]:
            copy.wait_send()
        halos[r].wait_send()
        backs[r].wait_send()


def home_kernel(capacity, chunk, places_ref, back_ref, tokens_ref, gain_ref, parts_ref, out_ref, total_ref):
    rounds, tok_dev = places_ref.shape
    slot_count = back_ref.shape[0]
    picks = None
    for hashing in range(rounds):
        slots = home_slots(places_ref[hashing : hashing + 1, :], tok_dev, chunk, hashing * capacity)
        ones = one_hot_rows(slots, slot_count)
        picks = ones if picks is None else picks + ones
    d_normal = dot_tn(picks, back_ref[...])
    x = tokens_ref[...].astype(F32)
    scale = lax.rsqrt(jnp.mean(x * x, axis=-1, keepdims=True) + EPS)
    t = d_normal * gain_ref[...]
    along = jnp.mean(x * t, axis=-1, keepdims=True)
    out_ref[...] = (t * scale - x * (scale * scale * scale * along)).astype(BF16)
    total_ref[...] = jnp.sum(parts_ref[:, 0, :], axis=0, keepdims=True)


def per_device(tokens, norm_gain, w_qk, w_v, cotangent, log_sums, bucket_order, token_position):
    devices = lax.axis_size("tok")
    me = lax.axis_index("tok")
    tok_dev, width = tokens.shape
    rounds, seq_len = bucket_order.shape
    heads = log_sums.shape[1]
    assert tok_dev == BLOCK
    capacity = 5 * tok_dev // (4 * devices)
    kinds = max(2, rounds)
    chunk = -(-kinds * capacity // 8) * 8
    slots = devices * chunk
    grad_scale = 1.0 / math.sqrt(seq_len)
    gain_row = norm_gain.reshape(1, width)
    my_order = lax.dynamic_slice_in_dim(bucket_order, me * tok_dev, tok_dev, axis=1).reshape(
        rounds, 1, tok_dev
    )
    outgoing = pl.pallas_call(
        functools.partial(dispatch_kernel, devices, capacity, chunk),
        out_shape=[jax.ShapeDtypeStruct((slots, width), BF16)] * rounds,
        in_specs=whole(3),
        out_specs=whole(rounds),
        compiler_params=params(),
        name="dispatch",
    )(token_position, tokens, cotangent)

    def low(*shape):
        return pltpu.VMEM(shape, BF16)

    per_round = (rounds, tok_dev, width)
    weights, rows_out, gain_slices = pl.pallas_call(
        functools.partial(core_kernel, heads, capacity, chunk, devices // 3, grad_scale),
        out_shape=[
            jax.ShapeDtypeStruct((width, 2 * width), BF16),
            jax.ShapeDtypeStruct((slots, width), BF16),
            jax.ShapeDtypeStruct((devices, 8, 128), F32),
        ],
        in_specs=whole(5) + [pl.BlockSpec(memory_space=pl.ANY)] * rounds,
        out_specs=whole(3),
        scratch_shapes=[
            low(rounds, devices, chunk, width),
            *[low(*per_round)] * 6,
            *[low(tok_dev, width)] * 2,
            *[pltpu.VMEM(per_round, F32)] * 3,
            *[low(rounds, tok_dev, 2 * width)] * 2,
            *[low(tok_dev, width)] * 2,
            low(*per_round),
            pltpu.VMEM((width, 2 * width), F32),
            pltpu.SemaphoreType.DMA((rounds, devices - 1)),
            pltpu.SemaphoreType.DMA((rounds, devices - 1)),
            pltpu.SemaphoreType.DMA((rounds,)),
            pltpu.SemaphoreType.DMA((2, rounds)),
            pltpu.SemaphoreType.DMA((2, rounds)),
        ],
        compiler_params=params(collective_id=0, has_side_effects=True),
        name="core",
    )(
        my_order, gain_row, w_qk, w_v, log_sums,
        *[rows.reshape(devices, chunk, width) for rows in outgoing],
    )
    grads = lax.psum_scatter(weights, "tok", scatter_dimension=0, tiled=True).astype(F32)
    own = width // devices
    rows_back, gain_back = exchange(
        [rows_out.reshape(devices, chunk, width), gain_slices], collective_id=1
    )
    d_tokens, d_gain = pl.pallas_call(
        functools.partial(home_kernel, capacity, chunk),
        out_shape=[
            jax.ShapeDtypeStruct((tok_dev, width), BF16),
            jax.ShapeDtypeStruct((1, 128), F32),
        ],
        in_specs=whole(5),
        out_specs=whole(2),
        compiler_params=params(),
        name="home",
    )(token_position, rows_back.reshape(slots, width), tokens, gain_row, gain_back)
    return (d_tokens, d_gain[0, :own], grads[:, :width], grads[:, width:])


def solution(mesh):
    in_specs = (
        P(("groups", "tok"), None),
        P(),
        P(),
        P(),
        P(("groups", "tok"), None),
        P(None, None, ("groups", "tok")),
        P(None, "groups"),
        P(None, ("groups", "tok")),
    )
    out_specs = (
        P(("groups", "tok"), None),
        P(("groups", "tok")),
        P(("groups", "tok"), None),
        P(("groups", "tok"), None),
    )
    return jax.shard_map(
        per_device, mesh=mesh, in_specs=in_specs, out_specs=out_specs, check_vma=False
    )
```

time: 249 us -> 214 us (0.86)
  waiting for transfers between devices: 54.5 us -> 27.7 us
  local copies, waits for them, and re-layouts: 11.4 us -> 4.26 us
  other arithmetic: 4.12 us -> 0 us
  Pallas kernels: 160 us -> 164 us
    pallas_call x4 -> x1, Pallas kernels: 42.4 us -> 94.3 us  [per_device(): pl.pallas_call(functools.partial(core_kernel, heads, capacity, chunk, dev...]
    pallas_call x2 -> x1, Pallas kernels: 110 us -> 63 us  [exchange(): pl.pallas_call(functools.partial(exchange_kernel, pieces), out_shape=[jax...]
    ppermute x2 -> x0, waiting for transfers between devices: 32 us -> none  [the longest x1 23.9 us: per_device(): returned = lax.ppermute(back, 'tok', [(b, a) for a, b in route])]
    reduce_scatter x1, waiting for transfers between devices: 22.5 us -> 27.7 us  [per_device(): lax.psum_scatter(weights, 'tok', scatter_dimension=0, tiled=True)]
    slice x1 -> x0, local copies, waits for them, and re-layouts: 3.47 us -> none  [per_device(): outbound[r].reshape(devices, chunk, width)]
    another operation x1 -> x0, other arithmetic: 3.47 us -> none  [per_device(): arrived = jnp.stack([a.reshape(slots, width) for a in arrived])]
  transfers between devices with their start and end apart: 3 -> 1, of which waited for: 3 -> 1; matrix products, arithmetic and copies ran while one was open for 1% -> 1% of each run, Pallas kernels for 25% -> 31%
where the time goes in v1:
time: 214 us; the launch traced here: 211 us
  Pallas kernels  164 us (77%)
  waiting for transfers between devices  27.7 us (13%)
  between operations  14.1 us (7%)
  local copies, waits for them, and re-layouts  4.26 us (2%)
    pallas_call x1, Pallas kernels, per_device(): pl.pallas_call(functools.partial(core_kernel, heads, capacity, chunk, dev...  94.3 us
    pallas_call x1, Pallas kernels, exchange(): pl.pallas_call(functools.partial(exchange_kernel, pieces), out_shape=[jax...  63 us
    reduce_scatter x1, waiting for transfers between devices, per_device(): lax.psum_scatter(weights, 'tok', scatter_dimension=0, tiled=True)  27.7 us
  transfers between devices with their start and end apart: 1, of which 1 were waited for; matrix products, arithmetic and copies ran while one was open for 1% of the time, Pallas kernels for 31%

profile of v1, /device:TPU:26, one launch (start us, length us, event | category | flops | bytes accessed | tf_op | source)
XLA Modules:
  0.0 210.5 jit_solution(13426653314373336634)
XLA Ops:
  7.2 0.0 copy-start
  7.2 0.0 reduce-scatter.2.cloned.1.call-start
  7.2 0.7 copy-done
  7.9 0.6 reshape.26.refs_0_
  8.5 3.9 %dispatch.1 = (bf16[640,1024]{1,0:T(8,128)(2,1)}, bf16[640,1024]{1,0:T(8,128)(2,1)}) custom-call(s32[2,256]{1,0:T(2,128)} %places_ref.3, bf16[256,1024]{1,0:T(8,128)(2,1)} %tokens_ref.3, bf16[256,1024]{1,0:T(8,128)(2,1)} %cot_ref.1), custom_call_target="tpu_custom_call" | custom-call | tf_op jit(solution)/shard_map/dispatch/pallas_call | solution.py:340
  12.4 94.3 %core.1 = (bf16[1024,2048]{1,0:T(8,128)(2,1)}, bf16[640,1024]{1,0:T(8,128)(2,1)}, f32[16,8,128]{2,1,0:T(8,128)}) custom-call(s32[2,1,256]{2,1,0:T(1,128)} %reshape.26.refs_0_, f32[1,1024]{1,0:T(1,128)} %bitcast.11, bf16[1024,1024]{1,0:T(8,128)(2,1)} %refs_2_.1, bf16[1024,1024]{1,0:T(8,128)(2,1)} %refs_3_.1, f32[2,8,256]{2,1,0:T(8,128)} %refs_4_.1, ...), custom_call_target="tpu_custom_call" | custom-call | tf_op jit(solution)/shard_map/core/pallas_call | solution.py:353
  106.7 0.0 reduce-scatter.2.cloned.1.call-update
  106.8 63.0 %shard_map.111 = (bf16[16,40,1024]{2,1,0:T(8,128)(2,1)}, f32[16,8,128]{2,1,0:T(8,128)}) custom-call(bf16[16,40,1024]{2,1,0:T(8,128)(2,1)} %bitcast.7, f32[16,8,128]{2,1,0:T(8,128)} %get-tuple-element.16.refs_1_), custom_call_target="tpu_custom_call" | custom-call | tf_op jit(solution)/shard_map/pallas_call | solution.py:112
  169.7 3.3 %home.1 = (bf16[256,1024]{1,0:T(8,128)(2,1)}, f32[1,128]{1,0:T(1,128)}) custom-call(s32[2,256]{1,0:T(2,128)} %places_ref.3, bf16[640,1024]{1,0:T(8,128)(2,1)} %bitcast.8, bf16[256,1024]{1,0:T(8,128)(2,1)} %tokens_ref.3, f32[1,1024]{1,0:T(1,128)} %bitcast.12, f32[16,8,128]{2,1,0:T(8,128)} %get-tuple-element.18.parts_ref), custom_call_target="tpu_custom_call" | custom-call | tf_op jit(solution)/shard_map/home/pallas_call | solution.py:388
  173.0 1.2 slice_bitcast_fusion
  174.2 27.7 %reduce-scatter.2.cloned.1.call-done = bf16[64,2048]{1,0:T(8,128)(2,1)} async-done(((bf16[1024,2048]{1,0:T(8,128)(2,1)}), bf16[64,2048]{1,0:T(8,128)(2,1)}) %reduce-scatter.2.cloned.1.call-update) | async-done | bytes 262160 | tf_op jit(solution)/shard_map/reduce_scatter | solution.py:383
  201.9 1.8 fusion
  (1 shorter events, 0.0 us)
Async XLA Ops:
  7.2 0.8 copy-start
  7.2 194.7 %reduce-scatter.2.cloned.1.call-start = ((), (), s32[]{:S(2)}) async-start(), calls=%async_computation.1 | async-start | bytes 4456448 | tf_op jit(solution)/shard_map/reduce_scatter | solution.py:383
Sparse Core Ops, SparseCore 0:
  106.9 94.9 reduce-scatter.1

commit v2 on v1

--- a/solution.py
+++ b/solution.py
@@ -10,7 +10,7 @@
 
 BLOCK = 256
 EPS = 1e-06
-VMEM_LIMIT = 60 * 1024 * 1024
+VMEM_LIMIT = 63 * 1024 * 1024
 MESH = pl.DeviceIdType.MESH
 F32 = jnp.float32
 BF16 = jnp.bfloat16
@@ -70,59 +70,6 @@
         out_refs[hashing][...] = rows.astype(BF16)
 
 
-def exchange_kernel(pieces, *refs):
-    sources, targets = refs[:pieces], refs[pieces : 2 * pieces]
-    send_sem, recv_sem, own_sem = refs[2 * pieces :]
-    devices = lax.axis_size("tok")
-    me = lax.axis_index("tok")
-    barrier = pltpu.get_barrier_semaphore()
-    for step in range(1, devices):
-        peer = lax.rem(me + step, devices)
-        pl.semaphore_signal(barrier, inc=1, device_id={"tok": peer}, device_id_type=MESH)
-    own = [
-        pltpu.make_async_copy(sources[i].at[me], targets[i].at[me], own_sem.at[i])
-        for i in range(pieces)
-    ]
-    for copy in own:
-        copy.start()
-    pl.semaphore_wait(barrier, devices - 1)
-    copies = []
-    for i in range(pieces):
-        for step in range(1, devices):
-            peer = lax.rem(me + step, devices)
-            copy = pltpu.make_async_remote_copy(
-                src_ref=sources[i].at[peer],
-                dst_ref=targets[i].at[me],
-                send_sem=send_sem.at[i, step - 1],
-                recv_sem=recv_sem.at[i, step - 1],
-                device_id={"tok": peer},
-                device_id_type=MESH,
-            )
-            copy.start()
-            copies.append(copy)
-    for copy in own:
-        copy.wait()
-    for copy in copies:
-        copy.wait()
-
-
-def exchange(arrays, collective_id):
-    devices = lax.axis_size("tok")
-    pieces = len(arrays)
-    return pl.pallas_call(
-        functools.partial(exchange_kernel, pieces),
-        out_shape=[jax.ShapeDtypeStruct(a.shape, a.dtype) for a in arrays],
-        in_specs=[pl.BlockSpec(memory_space=pl.ANY)] * pieces,
-        out_specs=[pl.BlockSpec(memory_space=pl.ANY)] * pieces,
-        scratch_shapes=[
-            pltpu.SemaphoreType.DMA((pieces, devices - 1)),
-            pltpu.SemaphoreType.DMA((pieces, devices - 1)),
-            pltpu.SemaphoreType.DMA((pieces,)),
-        ],
-        compiler_params=pltpu.CompilerParams(collective_id=collective_id, has_side_effects=True),
-    )(*arrays)
-
-
 def normal_of(x, gain):
     return (x * lax.rsqrt(jnp.mean(x * x, axis=-1, keepdims=True) + EPS) * gain).astype(BF16)
 
@@ -133,16 +80,30 @@
     return (q * scale / math.sqrt(depth)).astype(BF16)
 
 
-def core_kernel(heads, capacity, chunk, ahead, grad_scale, *refs):
+def flipped(index, mask):
+    bit = 1
+    while bit <= mask:
+        if mask & bit:
+            index = index + bit * (1 - 2 * lax.rem(lax.div(index, bit), 2))
+        bit *= 2
+    return index
+
+
+def forwarding_order(masks):
+    return sorted(masks, key=lambda m: int(bin(m)[:1:-1].ljust(16, "0"), 2), reverse=True)
+
+
+def core_kernel(heads, capacity, chunk, back_chunk, ahead, grad_scale, *refs):
     rounds = refs[0].shape[0]
-    order_ref, gain_ref, qk_ref, v_ref, sums_ref = refs[:5]
-    outgoing = refs[5 : 5 + rounds]
-    weights_ref, out_ref, gain_out = refs[5 + rounds : 8 + rounds]
+    order_ref, gain_ref, qk_ref, v_ref, sums_ref, places_ref, tokens_ref = refs[:7]
+    outgoing = refs[7 : 7 + rounds]
+    d_tokens_ref, d_gain_ref, d_qk_ref, d_v_ref = refs[7 + rounds : 11 + rounds]
     (
         arrived, sorted_x, sorted_g, halo_x, normal, query, value, halo_q, halo_v,
-        d_query, d_key, d_value, back_out, back_in, query_low, value_low, rows_low, total,
-        send_sem, recv_sem, own_sem, halo_sem, back_sem,
-    ) = refs[8 + rounds :]
+        d_query, d_key, d_value, back_out, back_in, query_low, value_low, total,
+        rows_out, rows_back, gain_out, gain_back, weights, sums_in, sums_run,
+        send_sem, recv_sem, own_sem, halo_sem, back_sem, rows_sem, gain_sem, home_sem, sums_sem,
+    ) = refs[11 + rounds :]
     devices = lax.axis_size("tok")
     me = lax.axis_index("tok")
     right, left = lax.rem(me + 1, devices), lax.rem(me + devices - 1, devices)
@@ -196,6 +157,54 @@
             device_id_type=MESH,
         )
         for r in range(rounds)
+    ]
+
+
+    def to_all(source, target, sems):
+        copies = []
+        for step in range(1, devices):
+            peer = lax.rem(me + step, devices)
+            copies.append(
+                pltpu.make_async_remote_copy(
+                    src_ref=source.at[peer],
+                    dst_ref=target.at[me],
+                    send_sem=sems.at[0, step - 1],
+                    recv_sem=sems.at[1, step - 1],
+                    device_id={"tok": peer},
+                    device_id_type=MESH,
+                )
+            )
+        return copies
+
+    homeward = [to_all(rows_out.at[r], rows_back.at[r], rows_sem.at[r]) for r in range(rounds)]
+    homeward.append(to_all(gain_out, gain_back, gain_sem))
+    stay = [
+        pltpu.make_async_copy(rows_out.at[r, me], rows_back.at[r, me], home_sem.at[r])
+        for r in range(rounds)
+    ]
+    stay.append(pltpu.make_async_copy(gain_out.at[me], gain_back.at[me], home_sem.at[rounds]))
+
+    def send_home(r):
+        for copy in [*homeward[r], stay[r]]:
+            copy.start()
+
+    bits = devices.bit_length() - 1
+    first_slot = [devices - (devices >> k) for k in range(bits)]
+
+    def sums_copy(k, mask):
+        slot = first_slot[k] + (mask >> (k + 1))
+        source = weights.at[flipped(me, mask)] if k == 0 else sums_run.at[mask >> 1]
+        return pltpu.make_async_remote_copy(
+            src_ref=source,
+            dst_ref=sums_in.at[slot],
+            send_sem=sums_sem.at[0, slot],
+            recv_sem=sums_sem.at[1, slot],
+            device_id={"tok": flipped(me, 1 << k)},
+            device_id_type=MESH,
+        )
+
+    stages = [
+        {m: sums_copy(k, m) for m in range(1 << k, devices, 2 << k)} for k in range(bits)
     ]
     for copy in pieces[0]:
         copy.start()
@@ -253,7 +262,10 @@
         d_normal = dot_nt(query_low[...], qk_ref[...]) + dot_nt(value_low[...], v_ref[...])
         x = sorted_x[r].astype(F32)
         scaled = x * lax.rsqrt(jnp.mean(x * x, axis=-1, keepdims=True) + EPS)
-        rows_low[r] = d_normal.astype(BF16)
+        slots = sorted_slots(order_ref[r], rows, back_chunk, 0)
+        placed = dot_nn(one_hot_rows(slots, devices * back_chunk), d_normal.astype(BF16))
+        rows_out[r] = placed.astype(BF16).reshape(devices, back_chunk, width)
+        gain = jnp.sum(d_normal * scaled, axis=0, keepdims=True)
         for low, columns in (
             (query_low, slice(0, width)),
             (value_low, slice(width, 2 * width)),
@@ -264,8 +276,29 @@
             if r < rounds - 1:
                 total[:, columns] = grad
             else:
-                weights_ref[:, columns] = (grad * grad_scale).astype(BF16)
-        return jnp.sum(d_normal * scaled, axis=0, keepdims=True)
+                grad = (grad * grad_scale).astype(BF16)
+                weights[:, :, columns] = grad.reshape(devices, width // devices, width)
+            if columns.start == 0:
+                send_home(r)
+        return gain
+
+    def go_home():
+        for copy in stay:
+            copy.wait()
+        for copies in homeward:
+            for copy in copies:
+                copy.wait_recv()
+        d_normal = jnp.zeros((rows, width), F32)
+        for r in range(rounds):
+            slots = home_slots(places_ref[r : r + 1, :], rows, back_chunk, 0)
+            data = rows_back[r].reshape(devices * back_chunk, width)
+            d_normal += dot_tn(one_hot_rows(slots, devices * back_chunk), data)
+        x = tokens_ref[...].astype(F32)
+        scale = lax.rsqrt(jnp.mean(x * x, axis=-1, keepdims=True) + EPS)
+        t = d_normal * gain_ref[...]
+        along = jnp.mean(x * t, axis=-1, keepdims=True)
+        d_tokens_ref[...] = (t * scale - x * (scale * scale * scale * along)).astype(BF16)
+        d_gain_ref[...] = jnp.sum(gain_back[:, 0, :], axis=0, keepdims=True)
 
     for r in range(rounds):
         if r + 1 < rounds:
@@ -292,33 +325,40 @@
     gain_out[...] = jnp.zeros(gain_out.shape, F32)
     for device in range(devices):
         gain_out[device, 0:1, 0:share] = gain_total[:, device * share : (device + 1) * share]
-    out = jnp.zeros((slot_count, width), F32)
-    for r in range(rounds):
-        slots = sorted_slots(order_ref[r], rows, chunk, r * capacity)
-        out += dot_nn(one_hot_rows(slots, slot_count), rows_low[r])
-    out_ref[...] = out.astype(BF16)
+    for mask in forwarding_order(stages[0]):
+        stages[0][mask].start()
+    send_home(rounds)
+    for k in range(bits):
+        waiting = None
+        for mask in forwarding_order(stages[k]):
+            mine = mask - (1 << k)
+            stages[k][mask].wait_recv()
+            arrived_sum = sums_in[first_slot[k] + (mask >> (k + 1))].astype(F32)
+            before = weights[flipped(me, mine)] if k == 0 else sums_run[mine >> 1]
+            run = before.astype(F32) + arrived_sum
+            if k == bits - 1:
+                d_qk_ref[...] = run[:, :width]
+                d_v_ref[...] = run[:, width:]
+                continue
+            sums_run[mine >> 1] = run.astype(BF16)
+            if waiting is not None:
+                waiting.start()
+            waiting = stages[k + 1].get(mine)
+        if waiting is not None:
+            waiting.start()
+        if k == min(1, bits - 1):
+            go_home()
+    for stage in stages:
+        for copy in stage.values():
+            copy.wait_send()
+    for copies in homeward:
+        for copy in copies:
+            copy.wait_send()
     for r in range(rounds):
         for copy in pieces[r]:
             copy.wait_send()
         halos[r].wait_send()
         backs[r].wait_send()
-
-
-def home_kernel(capacity, chunk, places_ref, back_ref, tokens_ref, gain_ref, parts_ref, out_ref, total_ref):
-    rounds, tok_dev = places_ref.shape
-    slot_count = back_ref.shape[0]
-    picks = None
-    for hashing in range(rounds):
-        slots = home_slots(places_ref[hashing : hashing + 1, :], tok_dev, chunk, hashing * capacity)
-        ones = one_hot_rows(slots, slot_count)
-        picks = ones if picks is None else picks + ones
-    d_normal = dot_tn(picks, back_ref[...])
-    x = tokens_ref[...].astype(F32)
-    scale = lax.rsqrt(jnp.mean(x * x, axis=-1, keepdims=True) + EPS)
-    t = d_normal * gain_ref[...]
-    along = jnp.mean(x * t, axis=-1, keepdims=True)
-    out_ref[...] = (t * scale - x * (scale * scale * scale * along)).astype(BF16)
-    total_ref[...] = jnp.sum(parts_ref[:, 0, :], axis=0, keepdims=True)
 
 
 def per_device(tokens, norm_gain, w_qk, w_v, cotangent, log_sums, bucket_order, token_position):
@@ -329,8 +369,8 @@
     heads = log_sums.shape[1]
     assert tok_dev == BLOCK
     capacity = 5 * tok_dev // (4 * devices)
-    kinds = max(2, rounds)
-    chunk = -(-kinds * capacity // 8) * 8
+    chunk = -(-2 * capacity // 8) * 8
+    back_chunk = -(-capacity // 8) * 8
     slots = devices * chunk
     grad_scale = 1.0 / math.sqrt(seq_len)
     gain_row = norm_gain.reshape(1, width)
@@ -350,15 +390,19 @@
         return pltpu.VMEM(shape, BF16)
 
     per_round = (rounds, tok_dev, width)
-    weights, rows_out, gain_slices = pl.pallas_call(
-        functools.partial(core_kernel, heads, capacity, chunk, devices // 3, grad_scale),
+    share = width // devices
+    d_tokens, d_gain, d_qk, d_v = pl.pallas_call(
+        functools.partial(
+            core_kernel, heads, capacity, chunk, back_chunk, devices // 3, grad_scale
+        ),
         out_shape=[
-            jax.ShapeDtypeStruct((width, 2 * width), BF16),
-            jax.ShapeDtypeStruct((slots, width), BF16),
-            jax.ShapeDtypeStruct((devices, 8, 128), F32),
+            jax.ShapeDtypeStruct((tok_dev, width), BF16),
+            jax.ShapeDtypeStruct((1, 128), F32),
+            jax.ShapeDtypeStruct((share, width), F32),
+            jax.ShapeDtypeStruct((share, width), F32),
         ],
-        in_specs=whole(5) + [pl.BlockSpec(memory_space=pl.ANY)] * rounds,
-        out_specs=whole(3),
+        in_specs=whole(7) + [pl.BlockSpec(memory_space=pl.ANY)] * rounds,
+        out_specs=whole(4),
         scratch_shapes=[
             low(rounds, devices, chunk, width),
             *[low(*per_round)] * 6,
@@ -366,37 +410,29 @@
             *[pltpu.VMEM(per_round, F32)] * 3,
             *[low(rounds, tok_dev, 2 * width)] * 2,
             *[low(tok_dev, width)] * 2,
-            low(*per_round),
             pltpu.VMEM((width, 2 * width), F32),
+            *[low(rounds, devices, back_chunk, width)] * 2,
+            *[pltpu.VMEM((devices, 8, 128), F32)] * 2,
+            low(devices, share, 2 * width),
+            low(devices - 1, share, 2 * width),
+            low(devices // 2, share, 2 * width),
             pltpu.SemaphoreType.DMA((rounds, devices - 1)),
             pltpu.SemaphoreType.DMA((rounds, devices - 1)),
             pltpu.SemaphoreType.DMA((rounds,)),
             pltpu.SemaphoreType.DMA((2, rounds)),
             pltpu.SemaphoreType.DMA((2, rounds)),
+            pltpu.SemaphoreType.DMA((rounds, 2, devices - 1)),
+            pltpu.SemaphoreType.DMA((2, devices - 1)),
+            pltpu.SemaphoreType.DMA((rounds + 1,)),
+            pltpu.SemaphoreType.DMA((2, devices - 1)),
         ],
         compiler_params=params(collective_id=0, has_side_effects=True),
         name="core",
     )(
-        my_order, gain_row, w_qk, w_v, log_sums,
+        my_order, gain_row, w_qk, w_v, log_sums, token_position, tokens,
         *[rows.reshape(devices, chunk, width) for rows in outgoing],
     )
-    grads = lax.psum_scatter(weights, "tok", scatter_dimension=0, tiled=True).astype(F32)
-    own = width // devices
-    rows_back, gain_back = exchange(
-        [rows_out.reshape(devices, chunk, width), gain_slices], collective_id=1
-    )
-    d_tokens, d_gain = pl.pallas_call(
-        functools.partial(home_kernel, capacity, chunk),
-        out_shape=[
-            jax.ShapeDtypeStruct((tok_dev, width), BF16),
-            jax.ShapeDtypeStruct((1, 128), F32),
-        ],
-        in_specs=whole(5),
-        out_specs=whole(2),
-        compiler_params=params(),
-        name="home",
-    )(token_position, rows_back.reshape(slots, width), tokens, gain_row, gain_back)
-    return (d_tokens, d_gain[0, :own], grads[:, :width], grads[:, width:])
+    return (d_tokens, d_gain[0, :share], d_qk, d_v)
 
 
 def solution(mesh):

time: 214 us -> 182 us (0.85); the launches traced: 211 us -> 182 us
  waiting for transfers between devices: 27.7 us -> 0 us
  between operations: 14.1 us -> 0.65 us
  Pallas kernels: 164 us -> 174 us
  local copies, waits for them, and re-layouts: 4.26 us -> 7.66 us
    reduce_scatter x1 -> x0, waiting for transfers between devices: 27.7 us -> none  [per_device(): lax.psum_scatter(weights, 'tok', scatter_dimension=0, tiled=True)]
    pallas_call x3 -> x1, Pallas kernels: 161 us -> 170 us  [per_device(): pl.pallas_call(functools.partial(core_kernel, heads, capacity, chunk, bac...]
    unnamed x2 -> x5, local copies, waits for them, and re-layouts: 0.71 us -> 5.96 us
  transfers between devices with their start and end apart: 1 -> 0, of which waited for: 1 -> 0; matrix products, arithmetic and copies ran while one was open for 1% -> 0% of each run, Pallas kernels for 31% -> 0%
where the time goes in v2:
time: 182 us
  Pallas kernels  174 us (96%)
  local copies, waits for them, and re-layouts  7.66 us (4%)
    pallas_call x1, Pallas kernels, per_device(): pl.pallas_call(functools.partial(core_kernel, heads, capacity, chunk, bac...  170 us
    unnamed x5, local copies, waits for them, and re-layouts  5.96 us
    pallas_call x1, Pallas kernels, per_device(): pl.pallas_call(functools.partial(dispatch_kernel, devices, capacity, chun...  3.95 us

profile of v2, /device:TPU:26, one launch (start us, length us, event | category | flops | bytes accessed | tf_op | source)
XLA Modules:
  0.0 182.1 jit_solution(11154929085605377465)
XLA Ops:
  0.6 0.0 copy-start
  0.6 0.7 copy-done
  1.4 0.6 reshape.20.refs_0_
  2.0 4.0 %dispatch.1 = (bf16[640,1024]{1,0:T(8,128)(2,1)}, bf16[640,1024]{1,0:T(8,128)(2,1)}) custom-call(s32[2,256]{1,0:T(2,128)} %refs_5_.1, bf16[256,1024]{1,0:T(8,128)(2,1)} %refs_6_.1, bf16[256,1024]{1,0:T(8,128)(2,1)} %cot_ref.1), custom_call_target="tpu_custom_call" | custom-call | tf_op jit(solution)/shard_map/dispatch/pallas_call | solution.py:380
  5.9 169.9 %core.1 = (bf16[256,1024]{1,0:T(8,128)(2,1)}, f32[1,128]{1,0:T(1,128)}, f32[64,1024]{1,0:T(8,128)}, f32[64,1024]{1,0:T(8,128)}) custom-call(s32[2,1,256]{2,1,0:T(1,128)} %reshape.20.refs_0_, f32[1,1024]{1,0:T(1,128)} %bitcast.7, bf16[1024,1024]{1,0:T(8,128)(2,1)} %refs_2_.1, bf16[1024,1024]{1,0:T(8,128)(2,1)} %refs_3_.1, f32[2,8,256]{2,1,0:T(8,128)} %refs_4_.1, ...), custom_call_target="tpu_custom_call" | custom-call | tf_op jit(solution)/shard_map/core/pallas_call | solution.py:394
  175.8 1.1 slice_bitcast_fusion
  176.9 1.9 %copy.15 = bf16[256,1024]{1,0:T(8,128)(2,1)} copy(bf16[256,1024]{1,0:T(8,128)(2,1)} %get-tuple-element.20) | data formatting | bytes 1048576
  178.8 1.7 copy.16
  180.5 1.7 copy.17
  (1 shorter events, 0.0 us)
Async XLA Ops:
  0.6 0.8 copy-start

commit v3 on v2

--- a/solution.py
+++ b/solution.py
@@ -97,13 +97,13 @@
     rounds = refs[0].shape[0]
     order_ref, gain_ref, qk_ref, v_ref, sums_ref, places_ref, tokens_ref = refs[:7]
     outgoing = refs[7 : 7 + rounds]
-    d_tokens_ref, d_gain_ref, d_qk_ref, d_v_ref = refs[7 + rounds : 11 + rounds]
+    d_tokens_ref, d_gain_ref, d_weights_ref = refs[7 + rounds : 10 + rounds]
     (
         arrived, sorted_x, sorted_g, halo_x, normal, query, value, halo_q, halo_v,
         d_query, d_key, d_value, back_out, back_in, query_low, value_low, total,
         rows_out, rows_back, gain_out, gain_back, weights, sums_in, sums_run,
         send_sem, recv_sem, own_sem, halo_sem, back_sem, rows_sem, gain_sem, home_sem, sums_sem,
-    ) = refs[11 + rounds :]
+    ) = refs[10 + rounds :]
     devices = lax.axis_size("tok")
     me = lax.axis_index("tok")
     right, left = lax.rem(me + 1, devices), lax.rem(me + devices - 1, devices)
@@ -191,20 +191,21 @@
     bits = devices.bit_length() - 1
     first_slot = [devices - (devices >> k) for k in range(bits)]
 
-    def sums_copy(k, mask):
+    def sums_copy(half, k, mask):
         slot = first_slot[k] + (mask >> (k + 1))
-        source = weights.at[flipped(me, mask)] if k == 0 else sums_run.at[mask >> 1]
+        source = weights.at[half, flipped(me, mask)] if k == 0 else sums_run.at[half, mask >> 1]
         return pltpu.make_async_remote_copy(
             src_ref=source,
-            dst_ref=sums_in.at[slot],
-            send_sem=sums_sem.at[0, slot],
-            recv_sem=sums_sem.at[1, slot],
+            dst_ref=sums_in.at[half, slot],
+            send_sem=sums_sem.at[half, 0, slot],
+            recv_sem=sums_sem.at[half, 1, slot],
             device_id={"tok": flipped(me, 1 << k)},
             device_id_type=MESH,
         )
 
     stages = [
-        {m: sums_copy(k, m) for m in range(1 << k, devices, 2 << k)} for k in range(bits)
+        [{m: sums_copy(half, k, m) for m in range(1 << k, devices, 2 << k)} for half in range(2)]
+        for k in range(bits)
     ]
     for copy in pieces[0]:
         copy.start()
@@ -259,28 +260,43 @@
             pulled = (dk * scale - q * (scale * scale * scale * along)) / math.sqrt(depth)
             query_low[:, part] = (d_query[r, :, part] + pulled).astype(BF16)
         value_low[...] = (d_value[r] + back_in[r, :, width:].astype(F32)).astype(BF16)
-        d_normal = dot_nt(query_low[...], qk_ref[...]) + dot_nt(value_low[...], v_ref[...])
-        x = sorted_x[r].astype(F32)
-        scaled = x * lax.rsqrt(jnp.mean(x * x, axis=-1, keepdims=True) + EPS)
-        slots = sorted_slots(order_ref[r], rows, back_chunk, 0)
-        placed = dot_nn(one_hot_rows(slots, devices * back_chunk), d_normal.astype(BF16))
-        rows_out[r] = placed.astype(BF16).reshape(devices, back_chunk, width)
-        gain = jnp.sum(d_normal * scaled, axis=0, keepdims=True)
-        for low, columns in (
-            (query_low, slice(0, width)),
-            (value_low, slice(width, 2 * width)),
-        ):
-            grad = dot_tn(normal[r], low[...])
+
+        def row_gradients():
+            d_normal = dot_nt(query_low[...], qk_ref[...]) + dot_nt(value_low[...], v_ref[...])
+            x = sorted_x[r].astype(F32)
+            scaled = x * lax.rsqrt(jnp.mean(x * x, axis=-1, keepdims=True) + EPS)
+            slots = sorted_slots(order_ref[r], rows, back_chunk, 0)
+            placed = dot_nn(one_hot_rows(slots, devices * back_chunk), d_normal.astype(BF16))
+            rows_out[r] = placed.astype(BF16).reshape(devices, back_chunk, width)
+            return jnp.sum(d_normal * scaled, axis=0, keepdims=True)
+
+        def weight_gradients(half):
+            columns = slice(half * width, (half + 1) * width)
+            grad = dot_tn(normal[r], (query_low, value_low)[half][...])
             if r > 0:
                 grad += total[:, columns]
             if r < rounds - 1:
                 total[:, columns] = grad
             else:
                 grad = (grad * grad_scale).astype(BF16)
-                weights[:, :, columns] = grad.reshape(devices, width // devices, width)
-            if columns.start == 0:
-                send_home(r)
+                weights[half] = grad.reshape(devices, width // devices, width)
+
+        if r < rounds - 1:
+            gain = row_gradients()
+            weight_gradients(0)
+            send_home(r)
+            weight_gradients(1)
+        else:
+            weight_gradients(0)
+            weight_gradients(1)
+            start_sums(0)
+            gain = row_gradients()
+            start_sums(1)
         return gain
+
+    def start_sums(half):
+        for mask in forwarding_order(stages[0][half]):
+            stages[0][half][mask].start()
 
     def go_home():
         for copy in stay:
@@ -325,31 +341,30 @@
     gain_out[...] = jnp.zeros(gain_out.shape, F32)
     for device in range(devices):
         gain_out[device, 0:1, 0:share] = gain_total[:, device * share : (device + 1) * share]
-    for mask in forwarding_order(stages[0]):
-        stages[0][mask].start()
+    send_home(rounds - 1)
     send_home(rounds)
     for k in range(bits):
         waiting = None
-        for mask in forwarding_order(stages[k]):
-            mine = mask - (1 << k)
-            stages[k][mask].wait_recv()
-            arrived_sum = sums_in[first_slot[k] + (mask >> (k + 1))].astype(F32)
-            before = weights[flipped(me, mine)] if k == 0 else sums_run[mine >> 1]
-            run = before.astype(F32) + arrived_sum
-            if k == bits - 1:
-                d_qk_ref[...] = run[:, :width]
-                d_v_ref[...] = run[:, width:]
-                continue
-            sums_run[mine >> 1] = run.astype(BF16)
-            if waiting is not None:
-                waiting.start()
-            waiting = stages[k + 1].get(mine)
+        for half in range(2):
+            for mask in forwarding_order(stages[k][half]):
+                mine = mask - (1 << k)
+                stages[k][half][mask].wait_recv()
+                arrived_sum = sums_in[half, first_slot[k] + (mask >> (k + 1))].astype(F32)
+                before = weights[half, flipped(me, mine)] if k == 0 else sums_run[half, mine >> 1]
+                run = before.astype(F32) + arrived_sum
+                if k == bits - 1:
+                    d_weights_ref[:, half * width : (half + 1) * width] = run
+                    continue
+                sums_run[half, mine >> 1] = run.astype(BF16)
+                if waiting is not None:
+                    waiting.start()
+                waiting = stages[k + 1][half].get(mine)
         if waiting is not None:
             waiting.start()
         if k == min(1, bits - 1):
             go_home()
     for stage in stages:
-        for copy in stage.values():
+        for copy in [*stage[0].values(), *stage[1].values()]:
             copy.wait_send()
     for copies in homeward:
         for copy in copies:
@@ -391,18 +406,17 @@
 
     per_round = (rounds, tok_dev, width)
     share = width // devices
-    d_tokens, d_gain, d_qk, d_v = pl.pallas_call(
+    d_tokens, d_gain, d_weights = pl.pallas_call(
         functools.partial(
             core_kernel, heads, capacity, chunk, back_chunk, devices // 3, grad_scale
         ),
         out_shape=[
             jax.ShapeDtypeStruct((tok_dev, width), BF16),
             jax.ShapeDtypeStruct((1, 128), F32),
-            jax.ShapeDtypeStruct((share, width), F32),
-            jax.ShapeDtypeStruct((share, width), F32),
+            jax.ShapeDtypeStruct((share, 2 * width), F32),
         ],
         in_specs=whole(7) + [pl.BlockSpec(memory_space=pl.ANY)] * rounds,
-        out_specs=whole(4),
+        out_specs=whole(3),
         scratch_shapes=[
             low(rounds, devices, chunk, width),
             *[low(*per_round)] * 6,
@@ -413,9 +427,9 @@
             pltpu.VMEM((width, 2 * width), F32),
             *[low(rounds, devices, back_chunk, width)] * 2,
             *[pltpu.VMEM((devices, 8, 128), F32)] * 2,
-            low(devices, share, 2 * width),
-            low(devices - 1, share, 2 * width),
-            low(devices // 2, share, 2 * width),
+            low(2, devices, share, width),
+            low(2, devices - 1, share, width),
+            low(2, devices // 2, share, width),
             pltpu.SemaphoreType.DMA((rounds, devices - 1)),
             pltpu.SemaphoreType.DMA((rounds, devices - 1)),
             pltpu.SemaphoreType.DMA((rounds,)),
@@ -424,7 +438,7 @@
             pltpu.SemaphoreType.DMA((rounds, 2, devices - 1)),
             pltpu.SemaphoreType.DMA((2, devices - 1)),
             pltpu.SemaphoreType.DMA((rounds + 1,)),
-            pltpu.SemaphoreType.DMA((2, devices - 1)),
+            pltpu.SemaphoreType.DMA((2, 2, devices - 1)),
         ],
         compiler_params=params(collective_id=0, has_side_effects=True),
         name="core",
@@ -432,7 +446,7 @@
         my_order, gain_row, w_qk, w_v, log_sums, token_position, tokens,
         *[rows.reshape(devices, chunk, width) for rows in outgoing],
     )
-    return (d_tokens, d_gain[0, :share], d_qk, d_v)
+    return (d_tokens, d_gain[0, :share], d_weights[:, :width], d_weights[:, width:])
 
 
 def solution(mesh):

time: 182 us -> 181 us (level)
    unnamed x5 -> x3, local copies, waits for them, and re-layouts: 5.96 us -> 2.62 us
    slice x0 -> x1, local copies, waits for them, and re-layouts: none -> 1.87 us  [per_device(): d_weights[:, width:]]
where the time goes in v3:
time: 181 us
  Pallas kernels  174 us (96%)
  local copies, waits for them, and re-layouts  6.25 us (3%)
    pallas_call x1, Pallas kernels, per_device(): pl.pallas_call(functools.partial(core_kernel, heads, capacity, chunk, bac...  170 us
    pallas_call x1, Pallas kernels, per_device(): pl.pallas_call(functools.partial(dispatch_kernel, devices, capacity, chun...  3.94 us

profile of v3, /device:TPU:26, one launch (start us, length us, event | category | flops | bytes accessed | tf_op | source)
XLA Modules:
  0.0 180.6 jit_solution(2455821259921268599)
XLA Ops:
  0.6 0.0 copy-start
  0.6 0.7 copy-done
  1.4 0.6 reshape.20.refs_0_
  2.0 3.9 %dispatch.1 = (bf16[640,1024]{1,0:T(8,128)(2,1)}, bf16[640,1024]{1,0:T(8,128)(2,1)}) custom-call(s32[2,256]{1,0:T(2,128)} %refs_5_.1, bf16[256,1024]{1,0:T(8,128)(2,1)} %refs_6_.1, bf16[256,1024]{1,0:T(8,128)(2,1)} %cot_ref.1), custom_call_target="tpu_custom_call" | custom-call | tf_op jit(solution)/shard_map/dispatch/pallas_call | solution.py:395
  5.9 169.7 %core.1 = (bf16[256,1024]{1,0:T(8,128)(2,1)}, f32[1,128]{1,0:T(1,128)}, f32[64,2048]{1,0:T(8,128)}) custom-call(s32[2,1,256]{2,1,0:T(1,128)} %reshape.20.refs_0_, f32[1,1024]{1,0:T(1,128)} %bitcast.7, bf16[1024,1024]{1,0:T(8,128)(2,1)} %refs_2_.1, bf16[1024,1024]{1,0:T(8,128)(2,1)} %refs_3_.1, f32[2,8,256]{2,1,0:T(8,128)} %refs_4_.1, s32[2,256]{1,0:T(2,128)} %refs_5_.1, ...), custom_call_target="tpu_custom_call" | custom-call | tf_op jit(solution)/shard_map/core/pallas_call | solution.py:409
  175.7 1.2 slice_bitcast_fusion
  176.8 1.9 %fusion = (f32[64,1024]{1,0:T(8,128)}, f32[64,1024]{1,0:T(8,128)}) fusion(f32[64,2048]{1,0:T(8,128)} %get-tuple-element.13), kind=kLoop, calls=%fused_computation.2 | loop fusion | bytes 1048576 | tf_op jit(solution)/shard_map/slice | solution.py:449
  178.7 1.9 %copy.13 = bf16[256,1024]{1,0:T(8,128)(2,1)} copy(bf16[256,1024]{1,0:T(8,128)(2,1)} %get-tuple-element.20) | data formatting | bytes 1048576
  (1 shorter events, 0.0 us)
Async XLA Ops:
  0.6 0.8 copy-start
